TPU v7x, 32 devices: a whole 2x2x4 slice. The times are simulated.
32 devices in a mesh: nodes: 8 (over y, x, core), heads: 4 (over z).
Axes of the slice: x: 2, y: 2, z: 4, core: 2. Of those that a mesh axis runs over, the one named last changes fastest.
Arguments:
- grid_state: bfloat16 [8192, 1024], P('nodes', 'heads'), may hold values from -6 to 6
- mesh_state: bfloat16 [2048, 1024], P('nodes', 'heads'), may hold values from -6 to 6
- encoder_query: bfloat16 [1024, 512], P('nodes', 'heads'), may hold values from -0.1875 to 0.1875
- encoder_key: bfloat16 [1024, 512], P('nodes', 'heads'), may hold values from -0.1875 to 0.1875
- encoder_value: bfloat16 [1024, 512], P('nodes', 'heads'), may hold values from -0.1875 to 0.1875
- encoder_output: bfloat16 [512, 1024], P('heads', 'nodes'), may hold values from -0.25 to 0.25
- window_query: bfloat16 [1024, 512], P('nodes', 'heads'), may hold values from -0.1875 to 0.1875
- window_key: bfloat16 [1024, 512], P('nodes', 'heads'), may hold values from -0.1875 to 0.1875
- window_value: bfloat16 [1024, 512], P('nodes', 'heads'), may hold values from -0.1875 to 0.1875
- window_output: bfloat16 [512, 1024], P('heads', 'nodes'), may hold values from -0.25 to 0.25
- expand_weight: bfloat16 [1024, 2048], P('nodes', 'heads'), may hold values from -0.1875 to 0.1875
- shrink_weight: bfloat16 [2048, 1024], P('heads', 'nodes'), may hold values from -0.125 to 0.125
- decoder_query: bfloat16 [1024, 512], P('nodes', 'heads'), may hold values from -0.1875 to 0.1875
- decoder_key: bfloat16 [1024, 512], P('nodes', 'heads'), may hold values from -0.1875 to 0.1875
- decoder_value: bfloat16 [1024, 512], P('nodes', 'heads'), may hold values from -0.1875 to 0.1875
- decoder_output: bfloat16 [512, 1024], P('heads', 'nodes'), may hold values from -0.25 to 0.25
- encoder_blocks: int32 [16, 8], P('nodes'), may hold values from 0 to 63, as said below
- encoder_count: int32 [16], P('nodes'), may hold values from 2 to 8, as said below
- window_offsets: int32 [16, 4], P('nodes'), may hold values from -2 to 2, as said below
- decoder_blocks: int32 [64, 3], P('nodes'), may hold values from 0 to 15, as said below
- decoder_count: int32 [64], P('nodes'), may hold values from 1 to 3, as said below
Outputs:
- grid_out: bfloat16 [8192, 1024], P('nodes', 'heads')
- mesh_out: bfloat16 [2048, 1024], P('nodes', 'heads')
Inputs may be any that keep to these rules, and one draw needn't show every extreme that they name: `encoder_blocks`: row m names 8 different grid blocks; each lies among the grid blocks of the index of nodes that holds mesh block m, or in the nearer half of the grid blocks of the index on either side. The first encoder_count[m] slots of row m are live; every mesh block held by the first or last eighth of the indices of nodes has all 8 slots live. `window_offsets`: each row holds 4 different offsets, the first of them 0. `decoder_blocks`: row g names 3 different mesh blocks; each lies among the mesh blocks of the index of nodes that holds grid block g, or is the one block next to them on either side. The first decoder_count[g] slots of row g are live; every grid block of the first index of nodes has all 3 slots live.
All inputs are finite; a program needn't handle non-finite values.
Results may differ from a plain program's by a relative error of at most 0.012.
Values may be sent and summed in bfloat16 or wider, within the bound.
A program may use at most 64 MiB of HBM per device.

v0:
```python
import math

import jax
import jax.numpy as jnp
from jax import lax
from jax.sharding import PartitionSpec as P

HEAD_DIM = 64
TILE = 128


EPSILON = 1e-05


def with_halo(x, sides, width):
    for axis, dim in sides:
        size, length = (lax.axis_size(axis), x.shape[dim])
        up = [(i, (i + 1) % size) for i in range(size - 1)]
        down = [(j, i) for i, j in up]
        last = lax.slice_in_dim(x, length - width, length, axis=dim)
        first = lax.slice_in_dim(x, 0, width, axis=dim)
        before = lax.ppermute(last, axis, up)
        after = lax.ppermute(first, axis, down)
        x = jnp.concatenate([before, x, after], axis=dim)
    return x


def normalize(values):
    values = values.astype(jnp.float32)
    average = jnp.mean(values, axis=-1, keepdims=True)
    centred = values - average
    spread = jnp.mean(centred * centred, axis=-1, keepdims=True)
    return (centred * lax.rsqrt(spread + EPSILON)).astype(jnp.bfloat16)


def add_terms(source, totals, pieces):
    result = []
    for running, weight_piece in zip(totals, pieces):
        result.append(jnp.dot(source, weight_piece, preferred_element_type=jnp.float32))
    return tuple(result)


def column_terms(source, weight_piece):
    return jnp.dot(source, weight_piece, preferred_element_type=jnp.float32)


def attend(queries, key_rows, value_rows, key_mask):
    batch_size, row_count, column_count = queries.shape
    head_count = column_count // HEAD_DIM
    split_query = queries.reshape(batch_size, row_count, head_count, HEAD_DIM)
    split_key = key_rows.reshape(batch_size, key_rows.shape[1], head_count, HEAD_DIM)
    split_value = value_rows.reshape(batch_size, value_rows.shape[1], head_count, HEAD_DIM)
    scores = jnp.einsum(
        "bqhd,bkhd->bhqk", split_query, split_key, preferred_element_type=jnp.float32
    )
    scores = jnp.where(key_mask[:, None, None, :], scores, -1e30)
    highest = jnp.max(scores, axis=-1, keepdims=True)
    weights = jnp.exp(scores - highest)
    weights = (weights / jnp.sum(weights, axis=-1, keepdims=True)).astype(jnp.bfloat16)
    mixture = jnp.einsum(
        "bhqk,bkhd->bqhd", weights, split_value, preferred_element_type=jnp.float32
    )
    return mixture.reshape(batch_size, row_count, column_count).astype(jnp.bfloat16)


def attend_blocks(queries, key_rows, value_rows, key_mask):
    tile_count = queries.shape[0]
    group_size = math.gcd(tile_count, 4)

    def one_group(arguments):
        return attend(arguments[0], arguments[1], arguments[2], arguments[3])

    grouped = tuple(
        (
            member.reshape((tile_count // group_size, group_size) + member.shape[1:])
            for member in (queries, key_rows, value_rows, key_mask)
        )
    )
    return lax.map(one_group, grouped).reshape(queries.shape)


def pick_tiles(stacked, tile_count, chosen):
    column_count = stacked.shape[-1]
    tile_view = stacked.reshape(2, tile_count, TILE, column_count)
    picked = jnp.take(tile_view, chosen, axis=1)
    shaped = picked.reshape(2, chosen.shape[0], chosen.shape[1] * TILE, column_count)
    return (shaped[0], shaped[1])


def slot_mask(live_count, slot_total):
    live = jnp.arange(slot_total, dtype=jnp.int32)[None, :] < live_count[:, None]
    return jnp.repeat(live, TILE, axis=1)


def local(
    grid_state,
    mesh_state,
    encoder_query,
    encoder_key,
    encoder_value,
    encoder_output,
    window_query,
    window_key,
    window_value,
    window_output,
    expand_weight,
    shrink_weight,
    decoder_query,
    decoder_key,
    decoder_value,
    decoder_output,
    encoder_blocks,
    encoder_count,
    window_offsets,
    decoder_blocks,
    decoder_count,
):
    scaling = HEAD_DIM ** (-0.5)
    position = lax.axis_index("nodes")
    head_lane = lax.axis_index("heads")
    grid_rows = grid_state.shape[0]
    mesh_rows = mesh_state.shape[0]
    feature_count = mesh_state.shape[1]
    grid_tiles = grid_rows // TILE
    mesh_tiles = mesh_rows // TILE
    all_mesh_tiles = mesh_tiles * lax.axis_size("nodes")
    head_columns = encoder_key.shape[1]
    grid_blank = jnp.zeros((grid_rows, head_columns), jnp.float32)
    mesh_blank = jnp.zeros((mesh_rows, head_columns), jnp.float32)
    grid_full = lax.all_gather(grid_state, "heads", axis=1, tiled=True)
    grid_norm = normalize(grid_full)
    grid_key, grid_value, grid_query = add_terms(
        grid_norm,
        (grid_blank, grid_blank, grid_blank),
        (
            lax.all_gather(encoder_key, "nodes", axis=0, tiled=True),
            lax.all_gather(encoder_value, "nodes", axis=0, tiled=True),
            lax.all_gather(decoder_query, "nodes", axis=0, tiled=True),
        ),
    )
    grid_queries = (grid_query * scaling).astype(jnp.bfloat16)
    mesh_full = lax.all_gather(mesh_state, "heads", axis=1, tiled=True)
    mesh_norm = normalize(mesh_full)
    (mesh_query,) = add_terms(
        mesh_norm, (mesh_blank,), (lax.all_gather(encoder_query, "nodes", axis=0, tiled=True),)
    )
    mesh_queries = (mesh_query * scaling).astype(jnp.bfloat16)
    rim_tiles = grid_tiles // 2
    stacked = jnp.stack([grid_key.astype(jnp.bfloat16), grid_value.astype(jnp.bfloat16)])
    padded = with_halo(stacked, (("nodes", 1),), rim_tiles * TILE)
    local_index = encoder_blocks - (position * grid_tiles - rim_tiles)
    key_rows, value_rows = pick_tiles(padded, grid_tiles + 2 * rim_tiles, local_index)
    key_mask = slot_mask(encoder_count, encoder_blocks.shape[1])
    encoded = attend_blocks(
        mesh_queries.reshape(mesh_tiles, TILE, head_columns), key_rows, value_rows, key_mask
    ).reshape(mesh_rows, head_columns)
    encoder_terms = column_terms(
        encoded, lax.all_gather(encoder_output, "nodes", axis=1, tiled=True)
    )
    encoder_sum = lax.psum(encoder_terms.astype(jnp.bfloat16), "heads").astype(jnp.float32)
    mesh_one = (mesh_full.astype(jnp.float32) + encoder_sum).astype(jnp.bfloat16)
    norm_one = normalize(mesh_one)
    window_queries, window_keys, window_values = add_terms(
        norm_one,
        (mesh_blank, mesh_blank, mesh_blank),
        (
            lax.all_gather(window_query, "nodes", axis=0, tiled=True),
            lax.all_gather(window_key, "nodes", axis=0, tiled=True),
            lax.all_gather(window_value, "nodes", axis=0, tiled=True),
        ),
    )
    window_queries = (window_queries * scaling).astype(jnp.bfloat16)
    stacked = jnp.stack([window_keys.astype(jnp.bfloat16), window_values.astype(jnp.bfloat16)])
    padded = with_halo(stacked, (("nodes", 1),), mesh_rows)
    tile_here = jnp.arange(mesh_tiles, dtype=jnp.int32)[:, None]
    key_rows, value_rows = pick_tiles(
        padded, 3 * mesh_tiles, tile_here + mesh_tiles + window_offsets
    )
    reached = position * mesh_tiles + tile_here + window_offsets
    key_mask = jnp.repeat((reached >= 0) & (reached < all_mesh_tiles), TILE, axis=1)
    windowed = attend_blocks(
        window_queries.reshape(mesh_tiles, TILE, head_columns), key_rows, value_rows, key_mask
    ).reshape(mesh_rows, head_columns)
    window_terms = column_terms(
        windowed, lax.all_gather(window_output, "nodes", axis=1, tiled=True)
    )
    window_sum = lax.psum(window_terms.astype(jnp.bfloat16), "heads").astype(jnp.float32)
    mesh_two = (mesh_one.astype(jnp.float32) + window_sum).astype(jnp.bfloat16)
    norm_two = normalize(mesh_two)
    hidden_blank = jnp.zeros((mesh_rows, expand_weight.shape[1]), jnp.float32)
    (hidden,) = add_terms(
        norm_two, (hidden_blank,), (lax.all_gather(expand_weight, "nodes", axis=0, tiled=True),)
    )
    hidden = jax.nn.gelu(hidden, approximate=False).astype(jnp.bfloat16)
    hidden_terms = column_terms(hidden, lax.all_gather(shrink_weight, "nodes", axis=1, tiled=True))
    hidden_sum = lax.psum(hidden_terms.astype(jnp.bfloat16), "heads").astype(jnp.float32)
    mesh_three = (mesh_two.astype(jnp.float32) + hidden_sum).astype(jnp.bfloat16)
    mesh_out = lax.dynamic_slice_in_dim(mesh_three, head_lane * feature_count, feature_count, 1)
    norm_three = normalize(mesh_three)
    mesh_keys, mesh_values = add_terms(
        norm_three,
        (mesh_blank, mesh_blank),
        (
            lax.all_gather(decoder_key, "nodes", axis=0, tiled=True),
            lax.all_gather(decoder_value, "nodes", axis=0, tiled=True),
        ),
    )
    stacked = jnp.stack([mesh_keys.astype(jnp.bfloat16), mesh_values.astype(jnp.bfloat16)])
    padded = with_halo(stacked, (("nodes", 1),), TILE)
    local_index = decoder_blocks - (position * mesh_tiles - 1)
    key_rows, value_rows = pick_tiles(padded, mesh_tiles + 2, local_index)
    key_mask = slot_mask(decoder_count, decoder_blocks.shape[1])
    decoded = attend_blocks(
        grid_queries.reshape(grid_tiles, TILE, head_columns), key_rows, value_rows, key_mask
    ).reshape(grid_rows, head_columns)
    quarter = lax.all_to_all(decoded, "heads", split_axis=0, concat_axis=1, tiled=True)
    whole_output = lax.all_gather(decoder_output, "heads", axis=0, tiled=True)
    decoder_terms = column_terms(quarter, lax.all_gather(whole_output, "nodes", axis=1, tiled=True))
    quarter_rows = quarter.shape[0]
    base_rows = lax.dynamic_slice_in_dim(grid_full, head_lane * quarter_rows, quarter_rows, 0)
    updated = (base_rows.astype(jnp.float32) + decoder_terms).astype(jnp.bfloat16)
    grid_out = lax.all_to_all(updated, "heads", split_axis=1, concat_axis=0, tiled=True)
    return (grid_out, mesh_out)


def solution(mesh):
    in_specs = (
        P("nodes", "heads"),
        P("nodes", "heads"),
        P("nodes", "heads"),
        P("nodes", "heads"),
        P("nodes", "heads"),
        P("heads", "nodes"),
        P("nodes", "heads"),
        P("nodes", "heads"),
        P("nodes", "heads"),
        P("heads", "nodes"),
        P("nodes", "heads"),
        P("heads", "nodes"),
        P("nodes", "heads"),
        P("nodes", "heads"),
        P("nodes", "heads"),
        P("heads", "nodes"),
        P("nodes", None),
        P("nodes"),
        P("nodes", None),
        P("nodes", None),
        P("nodes"),
    )
    out_specs = (P("nodes", "heads"), P("nodes", "heads"))
    return jax.shard_map(local, mesh=mesh, in_specs=in_specs, out_specs=out_specs, check_vma=False)
```

profile of v0, /device:TPU:3, one launch (start us, length us, event | category | flops | bytes accessed | tf_op | source)
XLA Modules:
  0.0 340.0 jit_solution(1236470662287655279)
XLA Ops:
  8.8 9.8 %all_gather.53 = bf16[1024,128]{1,0:T(8,128)(2,1)S(1)} all-gather(bf16[128,128]{1,0:T(8,128)(2,1)} %param.26), channel_id=1, replica_groups=mesh['nodes'=8,'heads'=4] {'nodes'}, dimensions={0}, use_global_device_ids=true | all-gather | bytes 294912 | tf_op jit(solution)/shard_map/all_gather | solution.py:136
  18.6 8.5 %all_gather.54 = bf16[1024,128]{1,0:T(8,128)(2,1)S(1)} all-gather(bf16[128,128]{1,0:T(8,128)(2,1)} %param.27), channel_id=1, replica_groups=mesh['nodes'=8,'heads'=4] {'nodes'}, dimensions={0}, use_global_device_ids=true | all-gather | bytes 294912 | tf_op jit(solution)/shard_map/all_gather | solution.py:137
  27.2 9.0 %all_gather.55 = bf16[1024,128]{1,0:T(8,128)(2,1)S(1)} all-gather(bf16[128,128]{1,0:T(8,128)(2,1)} %param.25), channel_id=1, replica_groups=mesh['nodes'=8,'heads'=4] {'nodes'}, dimensions={0}, use_global_device_ids=true | all-gather | bytes 294912 | tf_op jit(solution)/shard_map/all_gather | solution.py:145
  36.2 21.7 %all_gather.52 = bf16[256,1024]{1,0:T(8,128)(2,1)S(1)} all-gather(bf16[256,256]{1,0:T(8,128)(2,1)} %param.24), channel_id=1, replica_groups=mesh['nodes'=8,'heads'=4] {'heads'}, dimensions={1}, use_global_device_ids=true | all-gather | bytes 655360 | tf_op jit(solution)/shard_map/all_gather | solution.py:142
  60.2 6.1 %all-gather.5.cloned.1.call-done = bf16[1024,1024]{1,0:T(8,128)(2,1)} async-done(((bf16[1024,256]{1,0:T(8,128)(2,1)}), bf16[1024,1024]{1,0:T(8,128)(2,1)}) %all-gather.5.cloned.1.call-update) | async-done | bytes 2097168 | tf_op jit(solution)/shard_map/all_gather | solution.py:130
  72.1 3.6 %collective-permute-start = (bf16[2,512,128]{2,1,0:T(8,128)(2,1)}, bf16[2,512,128]{2,1,0:T(8,128)(2,1)}, u32[]{:S(2)}, u32[]{:S(2)}) collective-permute-start(bf16[2,512,128]{2,1,0:T(8,128)(2,1)} %get-tuple-element.123), channel_id=1, source_target_pairs={{0,4},{4,8},{8,12},{12,16},{16,20},{20,24},{24,28},{1,5},{5,9},{9,... | collective-permute-start | bytes 786440 | tf_op jit(solution)/shard_map/ppermute | solution.py:22
  80.5 10.0 %all_gather.56 = bf16[128,1024]{1,0:T(8,128)(2,1)S(1)} all-gather(bf16[128,128]{1,0:T(8,128)(2,1)} %param.28), channel_id=1, replica_groups=mesh['nodes'=8,'heads'=4] {'nodes'}, dimensions={1}, use_global_device_ids=true | all-gather | bytes 294912 | tf_op jit(solution)/shard_map/all_gather | solution.py:158
  110.8 10.1 %all_gather.59 = bf16[1024,128]{1,0:T(8,128)(2,1)} all-gather(bf16[128,128]{1,0:T(8,128)(2,1)} %param.29), channel_id=1, replica_groups=mesh['nodes'=8,'heads'=4] {'nodes'}, dimensions={0}, use_global_device_ids=true | all-gather | bytes 294912 | tf_op jit(solution)/shard_map/all_gather | solution.py:167
  120.9 10.1 %all_gather.57 = bf16[1024,128]{1,0:T(8,128)(2,1)} all-gather(bf16[128,128]{1,0:T(8,128)(2,1)} %param.30), channel_id=1, replica_groups=mesh['nodes'=8,'heads'=4] {'nodes'}, dimensions={0}, use_global_device_ids=true | all-gather | bytes 294912 | tf_op jit(solution)/shard_map/all_gather | solution.py:168
  131.0 10.0 %all_gather.58 = bf16[1024,128]{1,0:T(8,128)(2,1)} all-gather(bf16[128,128]{1,0:T(8,128)(2,1)S(1)} %copy-done.11), channel_id=1, replica_groups=mesh['nodes'=8,'heads'=4] {'nodes'}, dimensions={0}, use_global_device_ids=true | all-gather | bytes 294912 | tf_op jit(solution)/shard_map/all_gather | solution.py:169
  141.0 8.8 %all_gather.60 = bf16[128,1024]{1,0:T(8,128)(2,1)S(1)} all-gather(bf16[128,128]{1,0:T(8,128)(2,1)S(1)} %copy-done.12), channel_id=1, replica_groups=mesh['nodes'=8,'heads'=4] {'nodes'}, dimensions={1}, use_global_device_ids=true | all-gather | bytes 294912 | tf_op jit(solution)/shard_map/all_gather | solution.py:185
  158.5 4.2 %collective-permute-done.3 = bf16[2,256,128]{2,1,0:T(8,128)(2,1)} collective-permute-done((bf16[2,256,128]{2,1,0:T(8,128)(2,1)S(1)}, bf16[2,256,128]{2,1,0:T(8,128)(2,1)}, u32[]{:S(2)}, u32[]{:S(2)}) %collective-permute-start.3) | collective-permute-done | bytes 131104 | tf_op jit(solution)/shard_map/ppermute | solution.py:23
  175.6 33.3 %all-reduce.6.cloned.1.call-done = bf16[256,1024]{1,0:T(8,128)(2,1)} async-done(((bf16[256,1024]{1,0:T(8,128)(2,1)}), bf16[256,1024]{1,0:T(8,128)(2,1)}) %all-reduce.6.cloned.1.call-update) | async-done | bytes 524304 | tf_op jit(solution)/shard_map/psum | solution.py:187
  210.6 11.7 %all-gather.9.cloned.1.call-done = bf16[512,1024]{1,0:T(8,128)(2,1)} async-done(((bf16[512,128]{1,0:T(8,128)(2,1)}), bf16[512,1024]{1,0:T(8,128)(2,1)}) %all-gather.9.cloned.1.call-update) | async-done | bytes 1048592 | tf_op jit(solution)/shard_map/all_gather | solution.py:195
  222.3 4.3 %convolution_convert_fusion.1 = bf16[256,1024]{1,0:T(8,128)(2,1)} fusion(bf16[512,1024]{1,0:T(8,128)(2,1)} %all-gather.9.cloned.1.call-done, bf16[1024,512]{1,0:T(8,128)(2,1)} %all-gather.7.cloned.1.call-done, bf16[256,1024]{1,0:T(8,128)(2,1)S(1)} %get-tuple-element.106, f32[256]{0:T(256)S(1)} %add_rsqrt_fusion.2, f32[256]{0:T(256)S(1)} %broadcast_multiply_fusion.2), kind=kOutput, calls=%fused_computation.44 | convolution fusion | flops 546701312 | bytes 3147776 | tf_op jit(solution)/shard_map/dot_general | solution.py:44
  226.7 12.6 %all_gather.66 = bf16[512,128]{1,0:T(8,128)(2,1)} all-gather(bf16[128,128]{1,0:T(8,128)(2,1)S(1)} %copy-done.13), channel_id=1, replica_groups=mesh['nodes'=8,'heads'=4] {'heads'}, dimensions={0}, use_global_device_ids=true | all-gather | bytes 163840 | tf_op jit(solution)/shard_map/all_gather | solution.py:217
  239.3 11.0 %all_gather.64 = bf16[1024,128]{1,0:T(8,128)(2,1)S(1)} all-gather(bf16[128,128]{1,0:T(8,128)(2,1)S(1)} %copy-done.14), channel_id=1, replica_groups=mesh['nodes'=8,'heads'=4] {'nodes'}, dimensions={0}, use_global_device_ids=true | all-gather | bytes 294912 | tf_op jit(solution)/shard_map/all_gather | solution.py:205
  250.3 9.3 %all_gather.63 = bf16[1024,128]{1,0:T(8,128)(2,1)S(1)} all-gather(bf16[128,128]{1,0:T(8,128)(2,1)S(1)} %copy-done.15), channel_id=1, replica_groups=mesh['nodes'=8,'heads'=4] {'nodes'}, dimensions={0}, use_global_device_ids=true | all-gather | bytes 294912 | tf_op jit(solution)/shard_map/all_gather | solution.py:204
  259.9 8.3 %all_gather.65 = bf16[1024,128]{1,0:T(8,128)(2,1)S(1)} all-gather(bf16[128,128]{1,0:T(8,128)(2,1)S(1)} %copy-done.16), channel_id=1, replica_groups=mesh['nodes'=8,'heads'=4] {'nodes'}, dimensions={0}, use_global_device_ids=true | all-gather | bytes 294912 | tf_op jit(solution)/shard_map/all_gather | solution.py:138
  277.0 3.6 %collective-permute-done.5 = bf16[2,128,128]{2,1,0:T(8,128)(2,1)S(1)} collective-permute-done((bf16[2,128,128]{2,1,0:T(8,128)(2,1)S(1)}, bf16[2,128,128]{2,1,0:T(8,128)(2,1)S(1)}, u32[]{:S(2)}, u32[]{:S(2)}) %collective-permute-start.5) | collective-permute-done | bytes 65568 | tf_op jit(solution)/shard_map/ppermute | solution.py:23
  285.5 13.0 %while.2 = (s32[]{:T(128)}, bf16[2,4,128,128]{3,2,1,0:T(8,128)(2,1)}, bf16[2,4,384,128]{3,2,1,0:T(8,128)(2,1)}, pred[2,4,384]{2,1,0:T(4,128)(4,1)S(1)}, bf16[2,4...) while((s32[]{:T(128)}, bf16[2,4,128,128]{3,2,1,0:T(8,128)(2,1)}, ...), condition=%wide.region_20.21_spmd, body=%wide.region_17.20_spmd.sunk | while | flops 102695296 | bytes 10498709 | solution.py:79
  298.5 4.3 %all-to-all-start = ((bf16[4,256,128]{2,1,0:T(8,128)(2,1)}), bf16[4,256,128]{2,1,0:T(8,128)(2,1)S(1)}, u32[]{:S(2)}, u32[]{:S(2)}) async-start(bf16[4,256,128]{2,1,0:T(8,128)(2,1)} %bitcast.146), calls=%async_computation | async-start | bytes 524288 | tf_op jit(solution)/shard_map/all_to_all | solution.py:216
  302.8 7.9 %all-to-all-done = bf16[4,256,128]{2,1,0:T(8,128)(2,1)S(1)} async-done(((bf16[4,256,128]{2,1,0:T(8,128)(2,1)}), bf16[4,256,128]{2,1,0:T(8,128)(2,1)S(1)}, u32[]{:S(2)}, u32[]{:S(2)}) %all-to-all-start) | async-done | bytes 262176 | tf_op jit(solution)/shard_map/all_to_all | solution.py:216
  318.5 13.3 %all-to-all-done.1 = bf16[256,4,256]{2,0,1:T(8,128)(2,1)S(1)} async-done(((bf16[256,4,256]{2,0,1:T(8,128)(2,1)}), bf16[256,4,256]{2,0,1:T(8,128)(2,1)S(1)}, u32[]{:S(2)}, u32[]{:S(2)}) %all-to-all-start.1) | async-done | bytes 524320 | tf_op jit(solution)/shard_map/all_to_all | solution.py:222
  (189 shorter events, 92.0 us)
Async XLA Ops:
  8.0 50.4 %copy-start.22 = (s32[2]{0:T(128)S(1)}, s32[2]{0:T(128)}, u32[]{:S(2)}) copy-start(s32[2]{0:T(128)} %param.40) | copy-start | bytes 28
  8.0 50.6 %copy-start.19 = (s32[2,4]{1,0:T(2,128)S(1)}, s32[2,4]{1,0:T(2,128)}, u32[]{:S(2)}) copy-start(s32[2,4]{1,0:T(2,128)} %param.41) | copy-start | bytes 100
  8.0 58.3 %all-gather.5.cloned.1.call-start = ((), (), s32[]{:S(2)}) async-start(), calls=%async_computation.2 | async-start | bytes 2621440 | tf_op jit(solution)/shard_map/all_gather | solution.py:130
  8.8 141.1 %all-reduce.4.cloned.1.call-start = ((), (), s32[]{:S(2)}) async-start(), calls=%async_computation.3 | async-start | bytes 1048576 | tf_op jit(solution)/shard_map/psum | solution.py:160
  72.1 19.1 %collective-permute-start = (bf16[2,512,128]{2,1,0:T(8,128)(2,1)}, bf16[2,512,128]{2,1,0:T(8,128)(2,1)}, u32[]{:S(2)}, u32[]{:S(2)}) collective-permute-start(bf16[2,512,128]{2,1,0:T(8,128)(2,1)} %get-tuple-element.123), channel_id=1, source_target_pairs={{0,4},{4,8},{8,12},{12,16},{16,20},{20,24},{24,28},{1,5},{5,9},{9,... | collective-permute-start | bytes 786440 | tf_op jit(solution)/shard_map/ppermute | solution.py:22
  75.7 15.5 %collective-permute-start.1 = (bf16[2,512,128]{2,1,0:T(8,128)(2,1)}, bf16[2,512,128]{2,1,0:T(8,128)(2,1)}, u32[]{:S(2)}, u32[]{:S(2)}) collective-permute-start(bf16[2,512,128]{2,1,0:T(8,128)(2,1)} %get-tuple-element.124), channel_id=1, source_target_pairs={{4,0},{8,4},{12,8},{16,12},{20,16},{24,20},{28,24},{5,1},{9,5},{13... | collective-permute-start | bytes 786440 | tf_op jit(solution)/shard_map/ppermute | solution.py:23
  108.6 32.4 %copy-start.12 = (bf16[128,128]{1,0:T(8,128)(2,1)S(1)}, bf16[128,128]{1,0:T(8,128)(2,1)}, u32[]{:S(2)}) copy-start(bf16[128,128]{1,0:T(8,128)(2,1)} %param.32) | copy-start | bytes 98308
  108.6 41.2 %copy-start.20 = (s32[8]{0:T(128)S(1)}, s32[8]{0:T(128)}, u32[]{:S(2)}) copy-start(s32[8]{0:T(128)} %reshape.221) | copy-start | bytes 100
  110.7 98.3 %all-reduce.6.cloned.1.call-start = ((), (), s32[]{:S(2)}) async-start(), calls=%async_computation.4 | async-start | bytes 1048576 | tf_op jit(solution)/shard_map/psum | solution.py:187
  152.3 5.5 %collective-permute-start.2 = (bf16[2,256,128]{2,1,0:T(8,128)(2,1)S(1)}, bf16[2,256,128]{2,1,0:T(8,128)(2,1)S(1)}, u32[]{:S(2)}, u32[]{:S(2)}) collective-permute-start(bf16[2,256,128]{2,1,0:T(8,128)(2,1)S(1)} %pad_maximum_fusion.4), channel_id=1, source_target_pairs={{0,4},{4,8},{8,12},{12,16},{16,20},{20,24},{24,28},{1,5},{5,9},{9,... | collective-permute-start | bytes 393224 | tf_op jit(solution)/shard_map/ppermute | solution.py:22
  155.4 7.3 %collective-permute-start.3 = (bf16[2,256,128]{2,1,0:T(8,128)(2,1)S(1)}, bf16[2,256,128]{2,1,0:T(8,128)(2,1)}, u32[]{:S(2)}, u32[]{:S(2)}) collective-permute-start(bf16[2,256,128]{2,1,0:T(8,128)(2,1)S(1)} %pad_maximum_fusion.4), channel_id=1, source_target_pairs={{4,0},{8,4},{12,8},{16,12},{20,16},{24,20},{28,24},{5,1},{9,5},{13... | collective-permute-start | bytes 393224 | tf_op jit(solution)/shard_map/ppermute | solution.py:23
  174.4 36.2 %all-gather.7.cloned.1.call-start = ((), (), s32[]{:S(2)}) async-start(), calls=%async_computation.5 | async-start | bytes 1179648 | tf_op jit(solution)/shard_map/all_gather | solution.py:192
  175.0 47.3 %all-gather.9.cloned.1.call-start = ((), (), s32[]{:S(2)}) async-start(), calls=%async_computation.6 | async-start | bytes 1179648 | tf_op jit(solution)/shard_map/all_gather | solution.py:195
  175.6 92.8 %all-reduce.8.cloned.1.call-start = ((), (), s32[]{:S(2)}) async-start(), calls=%async_computation.7 | async-start | bytes 1048576 | tf_op jit(solution)/shard_map/psum | solution.py:196
  210.5 28.8 %copy-start.14 = (bf16[128,128]{1,0:T(8,128)(2,1)S(1)}, bf16[128,128]{1,0:T(8,128)(2,1)}, u32[]{:S(2)}) copy-start(bf16[128,128]{1,0:T(8,128)(2,1)} %param.37) | copy-start | bytes 98308
  210.5 39.8 %copy-start.15 = (bf16[128,128]{1,0:T(8,128)(2,1)S(1)}, bf16[128,128]{1,0:T(8,128)(2,1)}, u32[]{:S(2)}) copy-start(bf16[128,128]{1,0:T(8,128)(2,1)} %param.36) | copy-start | bytes 98308
  210.5 49.1 %copy-start.17 = (s32[8,3]{0,1:T(4,128)S(1)}, s32[8,3]{0,1:T(4,128)}, u32[]{:S(2)}) copy-start(s32[8,3]{0,1:T(4,128)} %param.42) | copy-start | bytes 292
  210.6 49.3 %copy-start.16 = (bf16[128,128]{1,0:T(8,128)(2,1)S(1)}, bf16[128,128]{1,0:T(8,128)(2,1)}, u32[]{:S(2)}) copy-start(bf16[128,128]{1,0:T(8,128)(2,1)} %param.35) | copy-start | bytes 98308
  210.6 57.6 %copy-start.23 = (s32[8]{0:T(128)S(1)}, s32[8]{0:T(128)}, u32[]{:S(2)}) copy-start(s32[8]{0:T(128)} %param.43) | copy-start | bytes 100
  226.6 84.3 %all-gather.11.cloned.1.call-start = ((), (), s32[]{:S(2)}) async-start(), calls=%async_computation.8 | async-start | bytes 1179648 | tf_op jit(solution)/shard_map/all_gather | solution.py:218
  270.9 6.0 %collective-permute-start.4 = (bf16[2,128,128]{2,1,0:T(8,128)(2,1)S(1)}, bf16[2,128,128]{2,1,0:T(8,128)(2,1)S(1)}, u32[]{:S(2)}, u32[]{:S(2)}) collective-permute-start(bf16[2,128,128]{2,1,0:T(8,128)(2,1)S(1)} %get-tuple-element.125), channel_id=1, source_target_pairs={{0,4},{4,8},{8,12},{12,16},{16,20},{20,24},{24,28},{1,5},{5,9},{9,... | collective-permute-start | bytes 196616 | tf_op jit(solution)/shard_map/ppermute | solution.py:22
  274.1 6.5 %collective-permute-start.5 = (bf16[2,128,128]{2,1,0:T(8,128)(2,1)S(1)}, bf16[2,128,128]{2,1,0:T(8,128)(2,1)S(1)}, u32[]{:S(2)}, u32[]{:S(2)}) collective-permute-start(bf16[2,128,128]{2,1,0:T(8,128)(2,1)S(1)} %get-tuple-element.126), channel_id=1, source_target_pairs={{4,0},{8,4},{12,8},{16,12},{20,16},{24,20},{28,24},{5,1},{9,5},{13... | collective-permute-start | bytes 196616 | tf_op jit(solution)/shard_map/ppermute | solution.py:23
  298.5 12.2 %all-to-all-start = ((bf16[4,256,128]{2,1,0:T(8,128)(2,1)}), bf16[4,256,128]{2,1,0:T(8,128)(2,1)S(1)}, u32[]{:S(2)}, u32[]{:S(2)}) async-start(bf16[4,256,128]{2,1,0:T(8,128)(2,1)} %bitcast.146), calls=%async_computation | async-start | bytes 524288 | tf_op jit(solution)/shard_map/all_to_all | solution.py:216
  313.5 18.4 %all-to-all-start.1 = ((bf16[256,4,256]{2,0,1:T(8,128)(2,1)}), bf16[256,4,256]{2,0,1:T(8,128)(2,1)S(1)}, u32[]{:S(2)}, u32[]{:S(2)}) async-start(bf16[256,4,256]{2,0,1:T(8,128)(2,1)} %bitcast.110), calls=%async_computation.1 | async-start | bytes 1048576 | tf_op jit(solution)/shard_map/all_to_all | solution.py:222
  (17 other events, 88.6 us)
Sparse Core Ops, SparseCore 0:
  10.4 55.9 all-gather.4
  110.8 35.1 all-reduce.3
  174.5 34.3 all-reduce.5
  226.7 38.0 all-reduce.7
Sparse Core Ops, SparseCore 1:
  176.8 20.3 all-gather.6
  198.9 23.3 all-gather.8
  239.4 25.9 all-gather.10
where the time goes:
time: 342 us; the launch traced here: 340 us
  blocking collectives  139 us (41%)
  waiting for transfers between devices  82.1 us (24%)
  local copies, waits for them, and re-layouts  32.6 us (10%)
  matrix products  29.8 us (9%)
  starting transfers between devices  23.9 us (7%)
  other arithmetic  16 us (5%)
  between operations  16 us (5%)
    psum x1, waiting for transfers between devices, local(): lax.psum(window_terms.astype(jnp.bfloat16), 'heads').astype(jnp.float32)  33.3 us
    all_gather x1, blocking collectives, local(): mesh_full = lax.all_gather(mesh_state, 'heads', axis=1, tiled=True)  21.7 us
    all_to_all x1, waiting for transfers between devices, local(): lax.all_to_all(updated, 'heads', split_axis=1, concat_axis=0, tiled=True)  13.3 us
    all_gather x1, blocking collectives, local(): whole_output = lax.all_gather(decoder_output, 'heads', axis=0, tiled=True)  12.6 us
    all_gather x1, waiting for transfers between devices, local(): lax.all_gather(shrink_weight, 'nodes', axis=1, tiled=True)  11.7 us
    gather x6, local copies, waits for them, and re-layouts, pick_tiles(): picked = jnp.take(tile_view, chosen, axis=1)  11.5 us
    all_gather x1, blocking collectives, local(): lax.all_gather(decoder_value, 'nodes', axis=0, tiled=True)  11 us
    all_gather x1, blocking collectives, local(): lax.all_gather(window_query, 'nodes', axis=0, tiled=True)  10.1 us
  transfers between devices with their start and end apart: 15, of which 7 were waited for; matrix products, arithmetic and copies ran while one was open for 9% of the time, Pallas kernels for 0%

commit v1 on v0

v1 whole, which is shorter than its diff:
```python
import functools

import jax
import jax.numpy as jnp
from jax import lax
from jax.experimental import pallas as pl
from jax.experimental.pallas import tpu as pltpu
from jax.sharding import PartitionSpec as P

HEAD_DIM = 64
TILE = 128
EPSILON = 1e-05
PARTS = 4
MESH = pl.DeviceIdType.MESH
F32 = jnp.float32
BF16 = jnp.bfloat16


def normalize(values):
    average = jnp.mean(values, axis=-1, keepdims=True)
    centred = values - average
    spread = jnp.mean(centred * centred, axis=-1, keepdims=True)
    return (centred * lax.rsqrt(spread + EPSILON)).astype(BF16)


def dot(a, b):
    return jnp.dot(a, b, preferred_element_type=F32)


def dot_t(a, b):
    return lax.dot_general(a, b, (((1,), (1,)), ((), ())), preferred_element_type=F32)


def attend(query, key, value, mask):
    columns = query.shape[1]
    heads = columns // HEAD_DIM
    lane = lax.broadcasted_iota(jnp.int32, (1, columns), 1) // HEAD_DIM
    query = query.astype(F32)
    stacked = jnp.concatenate(
        [jnp.where(lane == i, query, 0.0) for i in range(heads)], axis=0
    ).astype(BF16)
    scores = dot_t(stacked, key)
    scores = jnp.where(mask, scores, -1e30)
    weights = jnp.exp(scores - jnp.max(scores, axis=-1, keepdims=True))
    weights = (weights * (1.0 / jnp.sum(weights, axis=-1, keepdims=True))).astype(BF16)
    mixed = dot(weights, value)
    rows = query.shape[0]
    result = mixed[:rows]
    for i in range(1, heads):
        result = jnp.where(lane == i, mixed[i * rows : (i + 1) * rows], result)
    return result.astype(BF16)


def kernel(count, lanes, gathers, *refs):
    N, H = count, lanes
    (eb, ec, wo, db, dc, grid_in, mesh_in) = refs[:7]
    refs = refs[7:]
    if gathers:
        a_in, b_in, c_in = refs[:3]
        grid_out, mesh_out = refs[3:5]
        refs = refs[5:]
        a_buf, b_buf, c_own, c_buf = refs[:4]
        refs = refs[4:]
    else:
        a_buf, b_buf, c_buf = refs[:3]
        grid_out, mesh_out = refs[3:5]
        refs = refs[5:]
    (
        grid_buf, kv, gq, mesh_buf, enc_buf, win_buf, two_buf, wkv, rs_src, rs_dst,
        three_buf, dkv, dec_buf, zs, zr, hs, hr, rs_s, rs_r,
    ) = refs[:19]
    if gathers:
        ns, nf, nr = refs[19:]
    scaling = HEAD_DIM ** (-0.5)
    n = lax.axis_index("nodes")
    h = lax.axis_index("heads")
    grid_rows, part_features = grid_in.shape
    mesh_rows = mesh_in.shape[0]
    chunk = grid_rows // PARTS
    rim = grid_rows // 2
    grid_tiles, mesh_tiles = grid_rows // TILE, mesh_rows // TILE
    cols = gq.shape[1]

    barrier = pltpu.get_barrier_semaphore()

    def greet(node, lane):
        pl.semaphore_signal(barrier, inc=1, device_id=(node, lane), device_id_type=MESH)

    node_steps = range(1, N) if gathers else (1, N - 1)
    for d in node_steps:
        greet(lax.rem(n + d, N), h)
    for d in range(1, H):
        greet(n, lax.rem(h + d, H))
    pl.semaphore_wait(barrier, len(node_steps) + H - 1)

    def copy(src, dst, send, recv, device):
        return pltpu.make_async_remote_copy(
            src_ref=src, dst_ref=dst, send_sem=send, recv_sem=recv,
            device_id=device, device_id_type=MESH,
        )

    def link(item, src, dst, slot, way):
        lane = h + 1 if way == 0 else h - 1
        return copy(src, dst, zs.at[way, item, slot], zr.at[item, slot], (n, lane))

    def chain_start(item, view, src=None):
        src = view(h) if src is None else src

        @pl.when(h + 1 < H)
        def _():
            link(item, src, view(h), h, 0).start()

        @pl.when(h > 0)
        def _():
            link(item, src, view(h), h, 1).start()

    def chain_step(item, view, s):
        @pl.when(h >= s)
        def _():
            a = h - s
            link(item, view(a), view(a), a, 1).wait_recv()

            @pl.when(h + 1 < H)
            def _():
                link(item, view(a), view(a), a, 0).start()

        @pl.when(h + s < H)
        def _():
            b = h + s
            link(item, view(b), view(b), b, 0).wait_recv()

            @pl.when(h > 0)
            def _():
                link(item, view(b), view(b), b, 1).start()

    def chain_drain(item, view):
        for s in range(H):

            @pl.when((h >= s) & (h + 1 < H))
            def _():
                link(item, view(h - s), view(h - s), h - s, 0).wait_send()

            @pl.when((h + s < H) & (h > 0))
            def _():
                link(item, view(h + s), view(h + s), h + s, 1).wait_send()

    beside = n + 1 - 2 * lax.rem(n, 2)

    def gather_start(item, view, src):
        for j in range(1, N // 2):
            peer = lax.rem(n + 2 * j, N)
            copy(src, view(n), ns.at[item, j], nr.at[item, n], (peer, h)).start()
        copy(src, view(n), nf.at[item, n], nr.at[item, n], (beside, h)).start()
        view(n)[...] = src[...]

    def gather_pass(item, view):
        for j in range(1, N // 2):
            m = lax.rem(n + N - 2 * j, N)
            forward = copy(view(m), view(m), nf.at[item, m], nr.at[item, m], (beside, h))
            forward.wait_recv()
            forward.start()

    def gather_wait(item, view):
        for j in range(N // 2):
            m = lax.rem(beside + N - 2 * j, N)
            copy(view(m), view(m), nf.at[item, m], nr.at[item, m], (beside, h)).wait_recv()

    def gather_drain(item, view):
        for j in range(N // 2):
            if j:
                copy(view(n), view(n), ns.at[item, j], nr.at[item, n], (beside, h)).wait_send()
            m = lax.rem(n + N - 2 * j, N)
            copy(view(m), view(m), nf.at[item, m], nr.at[item, m], (beside, h)).wait_send()

    def rows_of(buf, size):
        return lambda m: buf.at[pl.ds(pl.multiple_of(m * size, size), size), :]

    def grid_view(c):
        return lambda s: grid_buf.at[s, pl.ds(c * chunk, chunk), :]

    def dec_view(c):
        return lambda s: dec_buf.at[s, pl.ds(c * chunk, chunk), :]

    whole = lambda buf: (lambda s: buf.at[s])
    MESH_ITEM, OUT_ITEM, ENC_ITEM, WIN_ITEM, THREE_ITEM = range(PARTS, PARTS + 5)
    DEC_ITEM = PARTS + 5

    def halo(way, k, src, dst):
        node = n - 1 if way == 0 else n + 1
        return copy(src, dst, hs.at[way, k], hr.at[way, k], (node, h))

    def halo_ok(way):
        return n > 0 if way == 0 else n + 1 < N

    if gathers:
        shard = a_in.shape[0]
        a_view, b_view = rows_of(a_buf, shard), rows_of(b_buf, shard)
        c_view = lambda s: (
            lambda m: c_buf.at[s, pl.ds(pl.multiple_of(m * shard, shard), shard), :]
        )
        gather_start(0, a_view, a_in)
    for c in range(PARTS):
        chain_start(c, grid_view(c), grid_in.at[pl.ds(c * chunk, chunk), :])
    chain_start(MESH_ITEM, whole(mesh_buf), mesh_in)
    if gathers:
        gather_start(1, b_view, b_in)
        chain_start(OUT_ITEM, whole(c_own), c_in)
        c_own[h] = c_in[...]
    grid_buf[h] = grid_in[...]
    mesh_buf[h] = mesh_in[...]

    @pl.when(n == 0)
    def _():
        kv[0:rim, :] = jnp.zeros((rim, 2 * cols), BF16)
        wkv[0:mesh_rows, :] = jnp.zeros((mesh_rows, 2 * cols), BF16)
        dkv[0:TILE, :] = jnp.zeros((TILE, 2 * cols), BF16)

    @pl.when(n == N - 1)
    def _():
        kv[rim + grid_rows :, :] = jnp.zeros((rim, 2 * cols), BF16)
        wkv[2 * mesh_rows :, :] = jnp.zeros((mesh_rows, 2 * cols), BF16)
        dkv[TILE + mesh_rows :, :] = jnp.zeros((TILE, 2 * cols), BF16)

    for s in range(1, H):
        for c in range(PARTS):
            if s == 1 and c == 1 and gathers:
                gather_pass(0, a_view)
            if s < H - 1:
                chain_step(c, grid_view(c), s)
        if s < H - 1:
            chain_step(MESH_ITEM, whole(mesh_buf), s)
            if gathers:
                chain_step(OUT_ITEM, whole(c_own), s)
    if gathers:
        gather_wait(0, a_view)

    rim_parts = PARTS // 2

    def halo_enc(c):
        here = kv.at[pl.ds(rim + c * chunk, chunk), :]
        if c < rim_parts:
            return 0, c, here, kv.at[pl.ds(rim + grid_rows + c * chunk, chunk), :]
        k = c - rim_parts
        return 1, k, here, kv.at[pl.ds(k * chunk, chunk), :]

    def start_halo(args):
        @pl.when(halo_ok(args[0]))
        def _():
            halo(*args).start()

    def wait_halo(args):
        @pl.when(halo_ok(1 - args[0]))
        def _():
            halo(*args).wait_recv()

    def drain_halo(args):
        @pl.when(halo_ok(args[0]))
        def _():
            halo(*args).wait_send()

    def lanes_of(buf, rows):
        return jnp.concatenate([buf[i, rows, :] for i in range(H)], axis=1)

    for c in range(PARTS):
        chain_step(c, grid_view(c), H - 1)
        rows = pl.ds(c * chunk, chunk)
        normed = normalize(lanes_of(grid_buf, rows).astype(F32))
        made = dot(normed, a_buf[:, 0 : 3 * cols])
        kv[pl.ds(rim + c * chunk, chunk), :] = made[:, : 2 * cols].astype(BF16)
        gq[rows, :] = (made[:, 2 * cols :] * scaling).astype(BF16)
        start_halo(halo_enc(c))
    chain_step(MESH_ITEM, whole(mesh_buf), H - 1)
    everything = pl.ds(0, mesh_rows)
    mesh_full = lanes_of(mesh_buf, everything).astype(F32)
    mesh_q = (dot(normalize(mesh_full), a_buf[:, 3 * cols :]) * scaling).astype(BF16)
    if gathers:
        chain_step(OUT_ITEM, whole(c_own), H - 1)
        for s in range(H):
            gather_start(2 + s, c_view(s), c_own.at[s])
        gather_pass(1, b_view)
    for c in range(PARTS):
        wait_halo(halo_enc(c))

    def blocks_of(buf, start, width):
        rows = pl.ds(start * TILE, width * TILE)
        return buf[rows, 0:cols], buf[rows, cols : 2 * cols]

    def place_of(width):
        return lax.broadcasted_iota(jnp.int32, (1, width * TILE), 1) // TILE

    def live_slots(place, blocks, live_count):
        left = jnp.zeros(place.shape, jnp.int32)
        for s, block in enumerate(blocks):
            left = jnp.where(place == block, live_count - s, left)
        return left > 0

    base = n * grid_tiles - rim // TILE
    width = eb.shape[1]
    reach = (grid_rows + 2 * rim) // TILE
    place = place_of(reach)
    key, value = blocks_of(kv, 0, reach)
    for t in range(mesh_tiles):
        mask = live_slots(place, [eb[t, s] - base for s in range(width)], ec[t])
        enc_buf[h, pl.ds(t * TILE, TILE), :] = attend(
            mesh_q[t * TILE : (t + 1) * TILE], key, value, mask
        )
    chain_start(ENC_ITEM, whole(enc_buf))
    if gathers:
        for s in range(H):
            gather_pass(2 + s, c_view(s))
        gather_wait(1, b_view)
    for s in range(1, H):
        chain_step(ENC_ITEM, whole(enc_buf), s)
    if gathers:
        for s in range(H):
            gather_wait(2 + s, c_view(s))

    def out_weight(k, rows):
        return jnp.concatenate(
            [c_buf[i, rows, k * cols : (k + 1) * cols] for i in range(H)], axis=1
        )

    all_features = pl.ds(0, H * part_features)
    mesh_one = (
        mesh_full + dot_t(lanes_of(enc_buf, everything), out_weight(0, all_features))
    ).astype(BF16)
    made = dot(normalize(mesh_one.astype(F32)), b_buf[:, 0 : 3 * cols])
    window_q = (made[:, :cols] * scaling).astype(BF16)
    wkv[pl.ds(mesh_rows, mesh_rows), :] = made[:, cols:].astype(BF16)
    own = wkv.at[pl.ds(mesh_rows, mesh_rows), :]
    window_halo = [
        (0, rim_parts, own, wkv.at[pl.ds(2 * mesh_rows, mesh_rows), :]),
        (1, rim_parts, own, wkv.at[pl.ds(0, mesh_rows), :]),
    ]
    for args in window_halo:
        start_halo(args)
    for args in window_halo:
        wait_halo(args)
    width = wo.shape[1]
    for t in range(mesh_tiles):
        key, value = blocks_of(wkv, t, 2 * mesh_tiles + 1)
        place = place_of(2 * mesh_tiles + 1)
        reached = n * mesh_tiles + t - mesh_tiles + place
        chosen = live_slots(place, [mesh_tiles + wo[t, s] for s in range(width)], width)
        mask = chosen & (reached >= 0) & (reached < mesh_tiles * N)
        win_buf[h, pl.ds(t * TILE, TILE), :] = attend(
            window_q[t * TILE : (t + 1) * TILE], key, value, mask
        )
    chain_start(WIN_ITEM, whole(win_buf))
    for s in range(1, H):
        chain_step(WIN_ITEM, whole(win_buf), s)
    mesh_two = (
        mesh_one.astype(F32) + dot_t(lanes_of(win_buf, everything), out_weight(1, all_features))
    ).astype(BF16)
    for i in range(H):
        two_buf[i] = mesh_two[:, i * part_features : (i + 1) * part_features]
    units = (b_buf.shape[1] - 5 * cols) // 2
    first = 3 * cols
    hidden = dot(normalize(mesh_two.astype(F32)), b_buf[:, first : first + units])
    hidden = (0.5 * hidden * (1.0 + lax.erf(hidden * (0.5**0.5)))).astype(BF16)
    last = 5 * cols + units

    def term(lane):
        rows = pl.ds(pl.multiple_of(lane * part_features, part_features), part_features)
        return dot_t(hidden, b_buf[rows, last : last + units])

    def part_copy(d, lane):
        return copy(rs_src.at[d], rs_dst.at[d], rs_s.at[d], rs_r.at[d], (n, lane))

    for d in range(1, H):
        lane = lax.rem(h + d, H)
        rs_src[d] = term(lane).astype(BF16)
        part_copy(d, lane).start()
    total = two_buf[h].astype(F32) + term(h)
    for d in range(1, H):
        part_copy(d, lax.rem(h + d, H)).wait_recv()
        total = total + rs_dst[d].astype(F32)
    three = total.astype(BF16)
    three_buf[h] = three
    chain_start(THREE_ITEM, whole(three_buf))
    mesh_out[...] = three
    for s in range(1, H):
        chain_step(THREE_ITEM, whole(three_buf), s)
    mesh_norm = normalize(lanes_of(three_buf, everything).astype(F32))
    made = dot(mesh_norm, b_buf[:, first + units : last])
    dkv[pl.ds(TILE, mesh_rows), :] = made.astype(BF16)
    decoder_halo = [
        (0, rim_parts + 1, dkv.at[pl.ds(TILE, TILE), :], dkv.at[pl.ds(TILE + mesh_rows, TILE), :]),
        (1, rim_parts + 1, dkv.at[pl.ds(mesh_rows, TILE), :], dkv.at[pl.ds(0, TILE), :]),
    ]
    for args in decoder_halo:
        start_halo(args)
    for args in decoder_halo:
        wait_halo(args)
    base_mesh = n * mesh_tiles - 1
    width = db.shape[1]
    place = place_of(mesh_tiles + 2)
    key, value = blocks_of(dkv, 0, mesh_tiles + 2)
    per_part = grid_tiles // PARTS
    for c in range(PARTS):
        for u in range(per_part):
            g = c * per_part + u
            mask = live_slots(place, [db[g, s] - base_mesh for s in range(width)], dc[g])
            rows = pl.ds(g * TILE, TILE)
            dec_buf[h, rows, :] = attend(gq[rows, :], key, value, mask)
        chain_start(DEC_ITEM + c, dec_view(c))
    mine = pl.ds(pl.multiple_of(h * part_features, part_features), part_features)
    dec_weight = out_weight(2, mine)
    for s in range(1, H - 1):
        for c in range(PARTS):
            chain_step(DEC_ITEM + c, dec_view(c), s)
    for c in range(PARTS):
        chain_step(DEC_ITEM + c, dec_view(c), H - 1)
        rows = pl.ds(c * chunk, chunk)
        update = dot_t(lanes_of(dec_buf, rows), dec_weight)
        grid_out[rows, :] = (grid_in[rows, :].astype(F32) + update).astype(BF16)

    for c in range(PARTS):
        chain_drain(c, grid_view(c))
        chain_drain(DEC_ITEM + c, dec_view(c))
        drain_halo(halo_enc(c))
    chain_drain(MESH_ITEM, whole(mesh_buf))
    chain_drain(ENC_ITEM, whole(enc_buf))
    chain_drain(WIN_ITEM, whole(win_buf))
    chain_drain(THREE_ITEM, whole(three_buf))
    for args in window_halo + decoder_halo:
        drain_halo(args)
    for d in range(1, H):
        part_copy(d, lax.rem(h + d, H)).wait_send()
    if gathers:
        chain_drain(OUT_ITEM, whole(c_own))
        gather_drain(0, a_view)
        gather_drain(1, b_view)
        for s in range(H):
            gather_drain(2 + s, c_view(s))


def local(
    grid_state, mesh_state,
    encoder_query, encoder_key, encoder_value, encoder_output,
    window_query, window_key, window_value, window_output,
    expand_weight, shrink_weight,
    decoder_query, decoder_key, decoder_value, decoder_output,
    encoder_blocks, encoder_count, window_offsets, decoder_blocks, decoder_count,
):
    N, H = lax.axis_size("nodes"), lax.axis_size("heads")
    grid_rows, part = grid_state.shape
    mesh_rows = mesh_state.shape[0]
    shard, cols = encoder_key.shape
    features = part * H
    a = jnp.concatenate([encoder_key, encoder_value, decoder_query, encoder_query], axis=1)
    b = jnp.concatenate(
        [
            window_query, window_key, window_value, expand_weight,
            decoder_key, decoder_value, shrink_weight.T,
        ],
        axis=1,
    )
    c = jnp.concatenate([encoder_output.T, window_output.T, decoder_output.T], axis=1)
    gathers = N % 2 == 0 and shard % 16 == 0
    if not gathers:
        a = lax.all_gather(a, "nodes", axis=0, tiled=True)
        b = lax.all_gather(b, "nodes", axis=0, tiled=True)
        c = lax.all_gather(c, "nodes", axis=0, tiled=True)
        c = lax.all_gather(c, "heads", axis=0, tiled=False)
    V = pltpu.VMEM
    DMA = pltpu.SemaphoreType.DMA
    scratch = []
    if gathers:
        scratch += [
            V((features, a.shape[1]), BF16),
            V((features, b.shape[1]), BF16),
            V((H,) + c.shape, BF16),
            V((H, features, c.shape[1]), BF16),
        ]
    items = 2 * PARTS + 5
    scratch += [
        V((H, grid_rows, part), BF16),
        V((2 * grid_rows, 2 * cols), BF16),
        V((grid_rows, cols), BF16),
        V((H, mesh_rows, part), BF16),
        V((H, mesh_rows, cols), BF16),
        V((H, mesh_rows, cols), BF16),
        V((H, mesh_rows, part), BF16),
        V((3 * mesh_rows, 2 * cols), BF16),
        V((H, mesh_rows, part), BF16),
        V((H, mesh_rows, part), BF16),
        V((H, mesh_rows, part), BF16),
        V((mesh_rows + 2 * TILE, 2 * cols), BF16),
        V((H, grid_rows, cols), BF16),
        DMA((2, items, H)),
        DMA((items, H)),
        DMA((2, PARTS // 2 + 2)),
        DMA((2, PARTS // 2 + 2)),
        DMA((H,)),
        DMA((H,)),
    ]
    if gathers:
        scratch += [DMA((2 + H, N // 2)), DMA((2 + H, N)), DMA((2 + H, N))]
    smem = pl.BlockSpec(memory_space=pltpu.SMEM)
    vmem = pl.BlockSpec(memory_space=pltpu.VMEM)
    return pl.pallas_call(
        functools.partial(kernel, N, H, gathers),
        out_shape=(
            jax.ShapeDtypeStruct(grid_state.shape, BF16),
            jax.ShapeDtypeStruct(mesh_state.shape, BF16),
        ),
        in_specs=[smem] * 5 + [vmem] * 5,
        out_specs=(vmem, vmem),
        scratch_shapes=scratch,
        compiler_params=pltpu.CompilerParams(
            collective_id=0, has_side_effects=True, vmem_limit_bytes=56 * 2**20
        ),
    )(
        encoder_blocks, encoder_count, window_offsets, decoder_blocks, decoder_count,
        grid_state, mesh_state, a, b, c,
    )


def solution(mesh):
    rows, columns = P("nodes", "heads"), P("heads", "nodes")
    in_specs = (
        (rows,) * 5 + (columns,) + (rows,) * 3 + (columns,) + (rows, columns)
        + (rows,) * 3 + (columns,)
        + (P("nodes", None), P("nodes"), P("nodes", None), P("nodes", None), P("nodes"))
    )
    return jax.shard_map(
        local, mesh=mesh, in_specs=in_specs, out_specs=(rows, rows), check_vma=False
    )
```

time: 342 us -> 151 us (0.44)
  Pallas kernels: 0 us -> 139 us
  blocking collectives: 139 us -> 0 us
  waiting for transfers between devices: 82.1 us -> 0 us
  matrix products: 29.8 us -> 0 us
  starting transfers between devices: 23.9 us -> 0 us
  local copies, waits for them, and re-layouts: 32.6 us -> 9.68 us
  between operations: 16 us -> 0.75 us
  other arithmetic: 16 us -> 1.35 us
    all_gather x13 -> x0, blocking collectives: 139 us -> none  [the longest x1 21.7 us: local(): mesh_full = lax.all_gather(mesh_state, 'heads', axis=1, tiled=True)]
    pallas_call x0 -> x1, Pallas kernels: none -> 139 us  [local(): pl.pallas_call(functools.partial(kernel, N, H, gathers), out_shape=(jax.S...]
    psum x3 -> x0, waiting for transfers between devices: 33.3 us -> none  [the longest x1 33.3 us: local(): lax.psum(window_terms.astype(jnp.bfloat16), 'heads').astype(jnp.float32)]
    dot_general x18 -> x0, matrix products: 23.8 us -> none  [the longest x4 9.42 us: attend(): jnp.einsum('bhqk,bkhd->bqhd', weights, split_value, preferred_element_typ...]
    all_to_all x2 -> x0, waiting for transfers between devices: 21.2 us -> none  [the longest x1 13.3 us: local(): lax.all_to_all(updated, 'heads', split_axis=1, concat_axis=0, tiled=True)]
    all_gather x4 -> x0, waiting for transfers between devices: 17.9 us -> none  [the longest x1 11.7 us: local(): lax.all_gather(shrink_weight, 'nodes', axis=1, tiled=True)]
    ppermute x6 -> x0, starting transfers between devices: 15.8 us -> none  [the longest x3 9.85 us: with_halo(): before = lax.ppermute(last, axis, up)]
    gather x6 -> x0, local copies, waits for them, and re-layouts: 11.5 us -> none  [pick_tiles(): picked = jnp.take(tile_view, chosen, axis=1)]
  transfers between devices with their start and end apart: 15 -> 0, of which waited for: 7 -> 0; matrix products, arithmetic and copies ran while one was open for 9% -> 0% of each run, Pallas kernels for 0% -> 0%
where the time goes in v1:
time: 151 us; the launch traced here: 150 us
  Pallas kernels  139 us (92%)
  local copies, waits for them, and re-layouts  9.68 us (6%)
    pallas_call x1, Pallas kernels, local(): pl.pallas_call(functools.partial(kernel, N, H, gathers), out_shape=(jax.S...  139 us
    unnamed x43, local copies, waits for them, and re-layouts  9.68 us

profile of v1, /device:TPU:3, one launch (start us, length us, event | category | flops | bytes accessed | tf_op | source)
XLA Modules:
  0.0 150.3 jit_solution(8871264527859713085)
XLA Ops:
  0.6 1.3 copy.27.refs_3_
  2.0 0.9 copy.24
  2.9 0.0 copy-start.9
  2.9 0.1 copy.25
  3.0 0.6 copy-done.9
  3.6 0.1 copy.26
  3.7 0.7 pad_maximum_fusion.1.refs_9_
  4.4 0.1 copy-done.1
  4.5 0.1 copy.23
  4.7 0.6 copy-done.10
  5.3 0.0 copy-done.11
  5.4 0.8 copy-done.2
  6.2 0.7 copy-done.13
  7.0 0.0 copy-start.4
  7.0 0.0 copy-start.5
  7.0 0.7 copy-done.6
  7.7 0.0 copy-done.7
  7.7 0.0 copy-done.4
  7.8 0.0 copy-done.5
  7.8 0.7 pad_maximum_fusion
  8.4 0.8 copy-done
  9.2 138.5 %shard_map.212 = (bf16[1024,256]{1,0:T(8,128)(2,1)}, bf16[256,256]{1,0:T(8,128)(2,1)}) custom-call(s32[2,8]{1,0:T(2,128)} %refs_0_.1, s32[2]{0:T(128)} %refs_1_.1, s32[2,4]{1,0:T(2,128)} %refs_2_.1, s32[8,3]{1,0:T(8,128)} %copy.27.refs_3_, s32[8]{0:T(128)} %refs_4_.1, bf16[1024,256]{1,0:T(8,128)(2,1)} %refs_5_.1, bf16[256,256]{1,0:T(8,128)(2,1)} %refs_6_.1, ...), custom_call_target="tpu_custom_call" | custom-call | tf_op jit(solution)/shard_map/pallas_call | solution.py:502
  147.8 1.9 %copy.36 = bf16[1024,256]{1,0:T(8,128)(2,1)} copy(bf16[1024,256]{1,0:T(8,128)(2,1)} %get-tuple-element.6) | data formatting | bytes 1048576
  149.7 0.7 copy.37
  (22 shorter events, 0.1 us)
Async XLA Ops:
  2.0 0.9 copy-start.8
  2.9 0.8 copy-start.9
  3.6 0.9 copy-start.1
  4.5 0.8 copy-start.10
  4.5 0.8 copy-start.11
  4.5 0.8 copy-start.12
  5.3 0.9 copy-start.2
  6.2 0.8 copy-start.13
  6.2 0.8 copy-start.14
  7.0 0.8 copy-start.6
  7.0 0.8 copy-start.7
  7.0 0.8 copy-start.4
  7.0 0.8 copy-start.5
  8.4 0.8 copy-start
  147.8 1.9 %copy-start.3 = (bf16[256,256]{1,0:T(8,128)(2,1)S(1)}, bf16[256,256]{1,0:T(8,128)(2,1)}, u32[]{:S(2)}) copy-start(bf16[256,256]{1,0:T(8,128)(2,1)} %get-tuple-element.7) | copy-start | bytes 393220

commit v2 on v1

--- a/solution.py
+++ b/solution.py
@@ -53,18 +53,21 @@
 
 def kernel(count, lanes, gathers, *refs):
     N, H = count, lanes
-    (eb, ec, wo, db, dc, grid_in, mesh_in) = refs[:7]
-    refs = refs[7:]
-    if gathers:
-        a_in, b_in, c_in = refs[:3]
-        grid_out, mesh_out = refs[3:5]
-        refs = refs[5:]
-        a_buf, b_buf, c_own, c_buf = refs[:4]
-        refs = refs[4:]
+    eb, ec, wo, db, dc = refs[:5]
+    refs = refs[5:]
+    if gathers:
+        (
+            grid_in, mesh_in, eq_in, ek_in, ev_in, eo_in, wq_in, wk_in, wv_in, wout_in,
+            ex_in, sh_in, dq_in, dk_in, dv_in, dout_in,
+        ) = refs[:16]
+        grid_out, mesh_out = refs[16:18]
+        a_buf, b_buf, s_buf, o_own, o_buf, loads = refs[18:24]
+        refs = refs[24:]
     else:
-        a_buf, b_buf, c_buf = refs[:3]
-        grid_out, mesh_out = refs[3:5]
-        refs = refs[5:]
+        grid_in, mesh_in, a_buf, b_buf, s_buf, o_buf = refs[:6]
+        grid_out, mesh_out = refs[6:8]
+        loads = refs[8]
+        refs = refs[9:]
     (
         grid_buf, kv, gq, mesh_buf, enc_buf, win_buf, two_buf, wkv, rs_src, rs_dst,
         three_buf, dkv, dec_buf, zs, zr, hs, hr, rs_s, rs_r,
@@ -81,6 +84,30 @@
     grid_tiles, mesh_tiles = grid_rows // TILE, mesh_rows // TILE
     cols = gq.shape[1]
 
+    copies = []
+
+    def load(src, dst):
+        copies.append(pltpu.make_async_copy(src, dst, loads.at[len(copies)]))
+        copies[-1].start()
+
+    def placed(buf, size, column, src):
+        rows = pl.ds(pl.multiple_of(n * size, size), size)
+        load(src, buf.at[rows, pl.ds(column, src.shape[1])])
+
+    load(grid_in, grid_buf.at[h])
+    load(mesh_in, mesh_buf.at[h])
+    if gathers:
+        shard = ek_in.shape[0]
+        for k, src in enumerate((ek_in, ev_in, dq_in, eq_in)):
+            placed(a_buf, shard, k * cols, src)
+        for k, src in enumerate((eo_in, wout_in, dout_in)):
+            load(src, o_own.at[k, h])
+        column = 0
+        for src in (wq_in, wk_in, wv_in, ex_in, dk_in, dv_in):
+            placed(b_buf, shard, column, src)
+            column += src.shape[1]
+        load(sh_in, s_buf.at[:, pl.ds(pl.multiple_of(n * shard, shard), shard)])
+
     barrier = pltpu.get_barrier_semaphore()
 
     def greet(node, lane):
@@ -146,12 +173,15 @@
 
     beside = n + 1 - 2 * lax.rem(n, 2)
 
-    def gather_start(item, view, src):
+    def gather_start(item, view, src=None):
+        if src is None:
+            src = view(n)
+        else:
+            view(n)[...] = src[...]
         for j in range(1, N // 2):
             peer = lax.rem(n + 2 * j, N)
             copy(src, view(n), ns.at[item, j], nr.at[item, n], (peer, h)).start()
         copy(src, view(n), nf.at[item, n], nr.at[item, n], (beside, h)).start()
-        view(n)[...] = src[...]
 
     def gather_pass(item, view):
         for j in range(1, N // 2):
@@ -182,8 +212,9 @@
         return lambda s: dec_buf.at[s, pl.ds(c * chunk, chunk), :]
 
     whole = lambda buf: (lambda s: buf.at[s])
-    MESH_ITEM, OUT_ITEM, ENC_ITEM, WIN_ITEM, THREE_ITEM = range(PARTS, PARTS + 5)
-    DEC_ITEM = PARTS + 5
+    MESH_ITEM, ENC_ITEM, WIN_ITEM, THREE_ITEM = range(PARTS, PARTS + 4)
+    DEC_ITEM = PARTS + 4
+    OUT_ITEM = 2 * PARTS + 4
 
     def halo(way, k, src, dst):
         node = n - 1 if way == 0 else n + 1
@@ -192,22 +223,29 @@
     def halo_ok(way):
         return n > 0 if way == 0 else n + 1 < N
 
-    if gathers:
-        shard = a_in.shape[0]
+    for one in copies:
+        one.wait()
+    if gathers:
         a_view, b_view = rows_of(a_buf, shard), rows_of(b_buf, shard)
-        c_view = lambda s: (
-            lambda m: c_buf.at[s, pl.ds(pl.multiple_of(m * shard, shard), shard), :]
-        )
-        gather_start(0, a_view, a_in)
+        s_view = lambda m: s_buf.at[:, pl.ds(pl.multiple_of(m * shard, shard), shard)]
+        o_chain = lambda k: (lambda s: o_own.at[k, s])
+
+        def o_view(k, s):
+            return lambda m: o_buf.at[
+                k, pl.ds(s * cols, cols), pl.ds(pl.multiple_of(m * shard, shard), shard)
+            ]
+
+        gather_start(0, a_view)
+        chain_start(OUT_ITEM, o_chain(0))
     for c in range(PARTS):
-        chain_start(c, grid_view(c), grid_in.at[pl.ds(c * chunk, chunk), :])
-    chain_start(MESH_ITEM, whole(mesh_buf), mesh_in)
-    if gathers:
-        gather_start(1, b_view, b_in)
-        chain_start(OUT_ITEM, whole(c_own), c_in)
-        c_own[h] = c_in[...]
-    grid_buf[h] = grid_in[...]
-    mesh_buf[h] = mesh_in[...]
+        chain_start(c, grid_view(c))
+    chain_start(MESH_ITEM, whole(mesh_buf))
+    if gathers:
+        gather_start(1, b_view)
+        gather_start(2, s_view)
+
+    def out_items(k):
+        return [(3 + k * H + s, o_view(k, s), o_own.at[k, s]) for s in range(H)]
 
     @pl.when(n == 0)
     def _():
@@ -221,17 +259,20 @@
         wkv[2 * mesh_rows :, :] = jnp.zeros((mesh_rows, 2 * cols), BF16)
         dkv[TILE + mesh_rows :, :] = jnp.zeros((TILE, 2 * cols), BF16)
 
-    for s in range(1, H):
+    for s in range(1, H - 1):
+        if gathers:
+            chain_step(OUT_ITEM, o_chain(0), s)
         for c in range(PARTS):
             if s == 1 and c == 1 and gathers:
                 gather_pass(0, a_view)
-            if s < H - 1:
-                chain_step(c, grid_view(c), s)
-        if s < H - 1:
-            chain_step(MESH_ITEM, whole(mesh_buf), s)
-            if gathers:
-                chain_step(OUT_ITEM, whole(c_own), s)
-    if gathers:
+            chain_step(c, grid_view(c), s)
+        chain_step(MESH_ITEM, whole(mesh_buf), s)
+    if gathers:
+        chain_step(OUT_ITEM, o_chain(0), H - 1)
+        for item in out_items(0):
+            gather_start(*item)
+        for k in (1, 2):
+            chain_start(OUT_ITEM + k, o_chain(k))
         gather_wait(0, a_view)
 
     rim_parts = PARTS // 2
@@ -273,13 +314,21 @@
     everything = pl.ds(0, mesh_rows)
     mesh_full = lanes_of(mesh_buf, everything).astype(F32)
     mesh_q = (dot(normalize(mesh_full), a_buf[:, 3 * cols :]) * scaling).astype(BF16)
-    if gathers:
-        chain_step(OUT_ITEM, whole(c_own), H - 1)
-        for s in range(H):
-            gather_start(2 + s, c_view(s), c_own.at[s])
+    def pass_out(s):
+        if gathers:
+            for k in (1, 2):
+                chain_step(OUT_ITEM + k, o_chain(k), s)
+
+    for s in range(1, H - 2):
+        pass_out(s)
+    if gathers:
         gather_pass(1, b_view)
+        gather_pass(2, s_view)
+        for item in out_items(0):
+            gather_pass(*item[:2])
     for c in range(PARTS):
         wait_halo(halo_enc(c))
+    pass_out(H - 2)
 
     def blocks_of(buf, start, width):
         rows = pl.ds(start * TILE, width * TILE)
@@ -305,24 +354,20 @@
             mesh_q[t * TILE : (t + 1) * TILE], key, value, mask
         )
     chain_start(ENC_ITEM, whole(enc_buf))
-    if gathers:
-        for s in range(H):
-            gather_pass(2 + s, c_view(s))
+    pass_out(H - 1)
+    if gathers:
+        for k in (1, 2):
+            for item in out_items(k):
+                gather_start(*item)
         gather_wait(1, b_view)
     for s in range(1, H):
         chain_step(ENC_ITEM, whole(enc_buf), s)
     if gathers:
-        for s in range(H):
-            gather_wait(2 + s, c_view(s))
-
-    def out_weight(k, rows):
-        return jnp.concatenate(
-            [c_buf[i, rows, k * cols : (k + 1) * cols] for i in range(H)], axis=1
-        )
-
-    all_features = pl.ds(0, H * part_features)
+        for item in out_items(0):
+            gather_wait(*item[:2])
+
     mesh_one = (
-        mesh_full + dot_t(lanes_of(enc_buf, everything), out_weight(0, all_features))
+        mesh_full + dot(lanes_of(enc_buf, everything), o_buf[0])
     ).astype(BF16)
     made = dot(normalize(mesh_one.astype(F32)), b_buf[:, 0 : 3 * cols])
     window_q = (made[:, :cols] * scaling).astype(BF16)
@@ -334,6 +379,9 @@
     ]
     for args in window_halo:
         start_halo(args)
+    if gathers:
+        for item in out_items(1):
+            gather_pass(*item[:2])
     for args in window_halo:
         wait_halo(args)
     width = wo.shape[1]
@@ -349,20 +397,24 @@
     chain_start(WIN_ITEM, whole(win_buf))
     for s in range(1, H):
         chain_step(WIN_ITEM, whole(win_buf), s)
+    if gathers:
+        for item in out_items(1):
+            gather_wait(*item[:2])
     mesh_two = (
-        mesh_one.astype(F32) + dot_t(lanes_of(win_buf, everything), out_weight(1, all_features))
+        mesh_one.astype(F32) + dot(lanes_of(win_buf, everything), o_buf[1])
     ).astype(BF16)
     for i in range(H):
         two_buf[i] = mesh_two[:, i * part_features : (i + 1) * part_features]
-    units = (b_buf.shape[1] - 5 * cols) // 2
+    units = b_buf.shape[1] - 5 * cols
     first = 3 * cols
     hidden = dot(normalize(mesh_two.astype(F32)), b_buf[:, first : first + units])
     hidden = (0.5 * hidden * (1.0 + lax.erf(hidden * (0.5**0.5)))).astype(BF16)
-    last = 5 * cols + units
+    if gathers:
+        gather_wait(2, s_view)
 
     def term(lane):
-        rows = pl.ds(pl.multiple_of(lane * part_features, part_features), part_features)
-        return dot_t(hidden, b_buf[rows, last : last + units])
+        mine = pl.ds(pl.multiple_of(lane * part_features, part_features), part_features)
+        return dot(hidden, s_buf[:, mine])
 
     def part_copy(d, lane):
         return copy(rs_src.at[d], rs_dst.at[d], rs_s.at[d], rs_r.at[d], (n, lane))
@@ -379,10 +431,13 @@
     three_buf[h] = three
     chain_start(THREE_ITEM, whole(three_buf))
     mesh_out[...] = three
+    if gathers:
+        for item in out_items(2):
+            gather_pass(*item[:2])
     for s in range(1, H):
         chain_step(THREE_ITEM, whole(three_buf), s)
     mesh_norm = normalize(lanes_of(three_buf, everything).astype(F32))
-    made = dot(mesh_norm, b_buf[:, first + units : last])
+    made = dot(mesh_norm, b_buf[:, first + units :])
     dkv[pl.ds(TILE, mesh_rows), :] = made.astype(BF16)
     decoder_halo = [
         (0, rim_parts + 1, dkv.at[pl.ds(TILE, TILE), :], dkv.at[pl.ds(TILE + mesh_rows, TILE), :]),
@@ -393,27 +448,30 @@
     for args in decoder_halo:
         wait_halo(args)
     base_mesh = n * mesh_tiles - 1
-    width = db.shape[1]
+    width = db.shape[0]
     place = place_of(mesh_tiles + 2)
     key, value = blocks_of(dkv, 0, mesh_tiles + 2)
     per_part = grid_tiles // PARTS
     for c in range(PARTS):
         for u in range(per_part):
             g = c * per_part + u
-            mask = live_slots(place, [db[g, s] - base_mesh for s in range(width)], dc[g])
+            mask = live_slots(place, [db[s, g] - base_mesh for s in range(width)], dc[g])
             rows = pl.ds(g * TILE, TILE)
             dec_buf[h, rows, :] = attend(gq[rows, :], key, value, mask)
         chain_start(DEC_ITEM + c, dec_view(c))
     mine = pl.ds(pl.multiple_of(h * part_features, part_features), part_features)
-    dec_weight = out_weight(2, mine)
+    if gathers:
+        for item in out_items(2):
+            gather_wait(*item[:2])
+    dec_weight = o_buf[2, :, mine]
     for s in range(1, H - 1):
         for c in range(PARTS):
             chain_step(DEC_ITEM + c, dec_view(c), s)
     for c in range(PARTS):
         chain_step(DEC_ITEM + c, dec_view(c), H - 1)
         rows = pl.ds(c * chunk, chunk)
-        update = dot_t(lanes_of(dec_buf, rows), dec_weight)
-        grid_out[rows, :] = (grid_in[rows, :].astype(F32) + update).astype(BF16)
+        update = dot(lanes_of(dec_buf, rows), dec_weight)
+        grid_out[rows, :] = (grid_buf[h, rows, :].astype(F32) + update).astype(BF16)
 
     for c in range(PARTS):
         chain_drain(c, grid_view(c))
@@ -428,11 +486,13 @@
     for d in range(1, H):
         part_copy(d, lax.rem(h + d, H)).wait_send()
     if gathers:
-        chain_drain(OUT_ITEM, whole(c_own))
+        for k in range(3):
+            chain_drain(OUT_ITEM + k, o_chain(k))
+            for item in out_items(k):
+                gather_drain(*item[:2])
         gather_drain(0, a_view)
         gather_drain(1, b_view)
-        for s in range(H):
-            gather_drain(2 + s, c_view(s))
+        gather_drain(2, s_view)
 
 
 def local(
@@ -448,32 +508,45 @@
     mesh_rows = mesh_state.shape[0]
     shard, cols = encoder_key.shape
     features = part * H
-    a = jnp.concatenate([encoder_key, encoder_value, decoder_query, encoder_query], axis=1)
-    b = jnp.concatenate(
-        [
-            window_query, window_key, window_value, expand_weight,
-            decoder_key, decoder_value, shrink_weight.T,
-        ],
-        axis=1,
-    )
-    c = jnp.concatenate([encoder_output.T, window_output.T, decoder_output.T], axis=1)
-    gathers = N % 2 == 0 and shard % 16 == 0
-    if not gathers:
-        a = lax.all_gather(a, "nodes", axis=0, tiled=True)
-        b = lax.all_gather(b, "nodes", axis=0, tiled=True)
-        c = lax.all_gather(c, "nodes", axis=0, tiled=True)
-        c = lax.all_gather(c, "heads", axis=0, tiled=False)
+    gathers = N % 2 == 0 and shard % 128 == 0
     V = pltpu.VMEM
     DMA = pltpu.SemaphoreType.DMA
-    scratch = []
-    if gathers:
-        scratch += [
-            V((features, a.shape[1]), BF16),
-            V((features, b.shape[1]), BF16),
-            V((H,) + c.shape, BF16),
-            V((H, features, c.shape[1]), BF16),
+    units = expand_weight.shape[1]
+    if gathers:
+        weights = (
+            encoder_query, encoder_key, encoder_value, encoder_output,
+            window_query, window_key, window_value, window_output,
+            expand_weight, shrink_weight,
+            decoder_query, decoder_key, decoder_value, decoder_output,
+        )
+        scratch = [
+            V((features, 4 * cols), BF16),
+            V((features, 5 * cols + units), BF16),
+            V((units, features), BF16),
+            V((3, H, cols, shard), BF16),
+            V((3, H * cols, features), BF16),
         ]
-    items = 2 * PARTS + 5
+    else:
+        a = jnp.concatenate([encoder_key, encoder_value, decoder_query, encoder_query], axis=1)
+        b = jnp.concatenate(
+            [
+                window_query, window_key, window_value, expand_weight,
+                decoder_key, decoder_value,
+            ],
+            axis=1,
+        )
+        out = jnp.stack([encoder_output, window_output, decoder_output])
+        weights = (
+            lax.all_gather(a, "nodes", axis=0, tiled=True),
+            lax.all_gather(b, "nodes", axis=0, tiled=True),
+            lax.all_gather(shrink_weight, "nodes", axis=1, tiled=True),
+            lax.all_gather(
+                lax.all_gather(out, "nodes", axis=2, tiled=True), "heads", axis=1, tiled=True
+            ),
+        )
+        scratch = []
+    scratch += [DMA((16,))]
+    items = 2 * PARTS + 7
     scratch += [
         V((H, grid_rows, part), BF16),
         V((2 * grid_rows, 2 * cols), BF16),
@@ -496,24 +569,26 @@
         DMA((H,)),
     ]
     if gathers:
-        scratch += [DMA((2 + H, N // 2)), DMA((2 + H, N)), DMA((2 + H, N))]
+        scratch += [DMA((3 + 3 * H, N // 2)), DMA((3 + 3 * H, N)), DMA((3 + 3 * H, N))]
     smem = pl.BlockSpec(memory_space=pltpu.SMEM)
     vmem = pl.BlockSpec(memory_space=pltpu.VMEM)
+    hbm = pl.BlockSpec(memory_space=pl.ANY)
+    kept = [hbm] * len(weights) if gathers else [vmem] * len(weights)
     return pl.pallas_call(
         functools.partial(kernel, N, H, gathers),
         out_shape=(
             jax.ShapeDtypeStruct(grid_state.shape, BF16),
             jax.ShapeDtypeStruct(mesh_state.shape, BF16),
         ),
-        in_specs=[smem] * 5 + [vmem] * 5,
+        in_specs=[smem] * 5 + [hbm] * 2 + kept,
         out_specs=(vmem, vmem),
         scratch_shapes=scratch,
         compiler_params=pltpu.CompilerParams(
-            collective_id=0, has_side_effects=True, vmem_limit_bytes=56 * 2**20
+            collective_id=0, has_side_effects=True
         ),
     )(
-        encoder_blocks, encoder_count, window_offsets, decoder_blocks, decoder_count,
-        grid_state, mesh_state, a, b, c,
+        encoder_blocks, encoder_count, window_offsets, decoder_blocks.T, decoder_count,
+        grid_state, mesh_state, *weights,
     )
 
 

time: 151 us -> 136 us (0.901)
  local copies, waits for them, and re-layouts: 9.68 us -> 2.56 us
  Pallas kernels: 139 us -> 133 us
    unnamed x43 -> x4, local copies, waits for them, and re-layouts: 9.68 us -> 2.56 us
    pallas_call x1, Pallas kernels: 139 us -> 133 us  [local(): pl.pallas_call(functools.partial(kernel, N, H, gathers), out_shape=(jax.S...]
where the time goes in v2:
time: 136 us
  Pallas kernels  133 us (98%)
  local copies, waits for them, and re-layouts  2.56 us (2%)
    pallas_call x1, Pallas kernels, local(): pl.pallas_call(functools.partial(kernel, N, H, gathers), out_shape=(jax.S...  133 us

profile of v2, /device:TPU:3, one launch (start us, length us, event | category | flops | bytes accessed | tf_op | source)
XLA Modules:
  0.0 136.1 jit_solution(17684579020766005158)
XLA Ops:
  0.6 132.9 %shard_map.212 = (bf16[1024,256]{1,0:T(8,128)(2,1)}, bf16[256,256]{1,0:T(8,128)(2,1)}) custom-call(s32[2,8]{1,0:T(2,128)} %refs_0_.1, s32[2]{0:T(128)} %refs_1_.1, s32[2,4]{1,0:T(2,128)} %refs_2_.1, s32[3,8]{1,0:T(4,128)} %bitcast.1, s32[8]{0:T(128)} %refs_4_.1, bf16[1024,256]{1,0:T(8,128)(2,1)} %refs_5_.1, bf16[256,256]{1,0:T(8,128)(2,1)} %refs_6_.1, ...), custom_call_target="tpu_custom_call" | custom-call | tf_op jit(solution)/shard_map/pallas_call | solution.py:577
  133.5 0.0 copy-start
  133.6 1.9 %copy.25 = bf16[1024,256]{1,0:T(8,128)(2,1)} copy(bf16[1024,256]{1,0:T(8,128)(2,1)} %get-tuple-element.4) | data formatting | bytes 1048576
  135.5 0.0 copy-done
  135.5 0.7 copy.26
Async XLA Ops:
  133.5 1.9 %copy-start = (bf16[256,256]{1,0:T(8,128)(2,1)S(1)}, bf16[256,256]{1,0:T(8,128)(2,1)}, u32[]{:S(2)}) copy-start(bf16[256,256]{1,0:T(8,128)(2,1)} %get-tuple-element.5) | copy-start | bytes 393220

commit v3 on v2

--- a/solution.py
+++ b/solution.py
@@ -215,6 +215,13 @@
     MESH_ITEM, ENC_ITEM, WIN_ITEM, THREE_ITEM = range(PARTS, PARTS + 4)
     DEC_ITEM = PARTS + 4
     OUT_ITEM = 2 * PARTS + 4
+    TILE_ITEM = 2 * PARTS + 7
+
+    def tile_items(buf, first):
+        view = lambda t: (lambda s: buf.at[s, pl.ds(t * TILE, TILE), :])
+        return [(TILE_ITEM + first + t, view(t)) for t in range(mesh_tiles)]
+
+    enc_items, win_items = tile_items(enc_buf, 0), tile_items(win_buf, mesh_tiles)
 
     def halo(way, k, src, dst):
         node = n - 1 if way == 0 else n + 1
@@ -353,7 +360,7 @@
         enc_buf[h, pl.ds(t * TILE, TILE), :] = attend(
             mesh_q[t * TILE : (t + 1) * TILE], key, value, mask
         )
-    chain_start(ENC_ITEM, whole(enc_buf))
+        chain_start(*enc_items[t])
     pass_out(H - 1)
     if gathers:
         for k in (1, 2):
@@ -361,7 +368,8 @@
                 gather_start(*item)
         gather_wait(1, b_view)
     for s in range(1, H):
-        chain_step(ENC_ITEM, whole(enc_buf), s)
+        for item in enc_items:
+            chain_step(*item, s)
     if gathers:
         for item in out_items(0):
             gather_wait(*item[:2])
@@ -394,9 +402,10 @@
         win_buf[h, pl.ds(t * TILE, TILE), :] = attend(
             window_q[t * TILE : (t + 1) * TILE], key, value, mask
         )
-    chain_start(WIN_ITEM, whole(win_buf))
+        chain_start(*win_items[t])
     for s in range(1, H):
-        chain_step(WIN_ITEM, whole(win_buf), s)
+        for item in win_items:
+            chain_step(*item, s)
     if gathers:
         for item in out_items(1):
             gather_wait(*item[:2])
@@ -459,12 +468,15 @@
             rows = pl.ds(g * TILE, TILE)
             dec_buf[h, rows, :] = attend(gq[rows, :], key, value, mask)
         chain_start(DEC_ITEM + c, dec_view(c))
+        if c > 0:
+            chain_step(DEC_ITEM + c - 1, dec_view(c - 1), 1)
+    chain_step(DEC_ITEM + PARTS - 1, dec_view(PARTS - 1), 1)
     mine = pl.ds(pl.multiple_of(h * part_features, part_features), part_features)
     if gathers:
         for item in out_items(2):
             gather_wait(*item[:2])
     dec_weight = o_buf[2, :, mine]
-    for s in range(1, H - 1):
+    for s in range(2, H - 1):
         for c in range(PARTS):
             chain_step(DEC_ITEM + c, dec_view(c), s)
     for c in range(PARTS):
@@ -478,8 +490,8 @@
         chain_drain(DEC_ITEM + c, dec_view(c))
         drain_halo(halo_enc(c))
     chain_drain(MESH_ITEM, whole(mesh_buf))
-    chain_drain(ENC_ITEM, whole(enc_buf))
-    chain_drain(WIN_ITEM, whole(win_buf))
+    for item in enc_items + win_items:
+        chain_drain(*item)
     chain_drain(THREE_ITEM, whole(three_buf))
     for args in window_halo + decoder_halo:
         drain_halo(args)
@@ -546,7 +558,7 @@
         )
         scratch = []
     scratch += [DMA((16,))]
-    items = 2 * PARTS + 7
+    items = 2 * PARTS + 7 + 2 * (mesh_rows // TILE)
     scratch += [
         V((H, grid_rows, part), BF16),
         V((2 * grid_rows, 2 * cols), BF16),

time: 136 us -> 136 us (level)
  no operation moved by 1% of the time
where the time goes in v3:
time: 136 us
  Pallas kernels  132 us (97%)
  local copies, waits for them, and re-layouts  2.56 us (2%)
    pallas_call x1, Pallas kernels, local(): pl.pallas_call(functools.partial(kernel, N, H, gathers), out_shape=(jax.S...  132 us

profile of v3, /device:TPU:3, one launch (start us, length us, event | category | flops | bytes accessed | tf_op | source)
XLA Modules:
  0.0 135.7 jit_solution(14042941679151694726)
XLA Ops:
  0.6 132.5 %shard_map.212 = (bf16[1024,256]{1,0:T(8,128)(2,1)}, bf16[256,256]{1,0:T(8,128)(2,1)}) custom-call(s32[2,8]{1,0:T(2,128)} %refs_0_.1, s32[2]{0:T(128)} %refs_1_.1, s32[2,4]{1,0:T(2,128)} %refs_2_.1, s32[3,8]{1,0:T(4,128)} %bitcast.1, s32[8]{0:T(128)} %refs_4_.1, bf16[1024,256]{1,0:T(8,128)(2,1)} %refs_5_.1, bf16[256,256]{1,0:T(8,128)(2,1)} %refs_6_.1, ...), custom_call_target="tpu_custom_call" | custom-call | tf_op jit(solution)/shard_map/pallas_call | solution.py:589
  133.1 0.0 copy-start
  133.1 1.9 %copy.25 = bf16[1024,256]{1,0:T(8,128)(2,1)} copy(bf16[1024,256]{1,0:T(8,128)(2,1)} %get-tuple-element.4) | data formatting | bytes 1048576
  135.1 0.0 copy-done
  135.1 0.7 copy.26
Async XLA Ops:
  133.1 1.9 %copy-start = (bf16[256,256]{1,0:T(8,128)(2,1)S(1)}, bf16[256,256]{1,0:T(8,128)(2,1)}, u32[]{:S(2)}) copy-start(bf16[256,256]{1,0:T(8,128)(2,1)} %get-tuple-element.5) | copy-start | bytes 393220
